TPU v7x, 32 devices: a whole 2x2x4 slice. The times are simulated.
32 devices in a mesh: dp: 4 (over y, core), wide: 4 (over z), narrow: 2 (over x).
Axes of the slice: x: 2, y: 2, z: 4, core: 2. Of those that a mesh axis runs over, the one named last changes fastest.
Arguments:
- patches: bfloat16 [2, 38535168], P('narrow', ('dp', 'wide')), may hold values from -6 to 6
- visible: int32 [512, 49], P(('dp', 'wide')), may hold values from 0 to 195, as said below
- w_qkv: bfloat16 [768, 3, 768], P('narrow', None, 'wide'), may hold values from -0.3125 to 0.3125
- b_qv: bfloat16 [2, 768], P(None, 'wide'), may hold values from -3 to 3
- w_out: bfloat16 [768, 768], P('wide', 'narrow'), may hold values from -0.875 to 0.875
- b_out: bfloat16 [768], P('narrow'), may hold values from -2 to 2
- w_up: bfloat16 [768, 3072], P('narrow', 'wide'), may hold values from -0.21875 to 0.21875
- b_up: bfloat16 [3072], P('wide'), may hold values from -3 to 3
- w_down: bfloat16 [768, 3072], P('narrow', 'wide'), may hold values from -0.15625 to 0.15625
- b_down: bfloat16 [768], P('narrow'), may hold values from -2 to 2
- gain_one: bfloat16 [768], P('narrow'), may hold values from 0.099609375 to 1.8984375
- shift_one: bfloat16 [768], P('narrow'), may hold values from -2 to 2
- gain_two: bfloat16 [768], P('narrow'), may hold values from 0.099609375 to 1.8984375
- shift_two: bfloat16 [768], P('narrow'), may hold values from -2 to 2
- cotangent: bfloat16 [2, 9633792], P('narrow', ('dp', 'wide')), may hold values from -6 to 6
Outputs:
- block_output: bfloat16 [2, 9633792], P('narrow', ('dp', 'wide'))
- grad_patches: float32 [2, 38535168], P('narrow', ('dp', 'wide'))
- grad_wqkv: float32 [768, 3, 768], P('narrow', None, 'wide')
- grad_bqv: float32 [2, 768], P(None, 'wide')
- grad_wout: float32 [768, 768], P('wide', 'narrow')
- grad_bout: float32 [768], P('narrow')
- grad_wup: float32 [768, 3072], P('narrow', 'wide')
- grad_bup: float32 [3072], P('wide')
- grad_wdown: float32 [768, 3072], P('narrow', 'wide')
- grad_bdown: float32 [768], P('narrow')
- grad_gain1: float32 [768], P('narrow')
- grad_shift1: float32 [768], P('narrow')
- grad_gain2: float32 [768], P('narrow')
- grad_shift2: float32 [768], P('narrow')
Inputs may be any that keep to these rules, and one draw needn't show every extreme that they name: `visible`: each image's 49 indices are distinct and increasing.
All inputs are finite; a program needn't handle non-finite values.
Results may differ from a plain program's by a relative error of at most 0.012.
The roundings to bfloat16 on the way count: a program that leaves them out, or rounds other values in their place, can miss the bound.
Values may be sent and summed in bfloat16 or wider, within the bound.
No kernel may reach another device: no remote copies, remote signals or barrier semaphores. Data moves between devices by JAX's collectives and lax.ppermute only.
A program may use at most 256 MiB of HBM per device.

v0:
```python
from functools import partial
import jax
import jax.numpy as jnp
from jax import lax
from jax.sharding import PartitionSpec as P

D = 768
HEAD_DIM = 64
PATCHES = 196
VISIBLE = 49
epsilon = 1e-06


def narrow_product(acts, weight):
    return lax.psum_scatter(
        jnp.dot(acts, weight, preferred_element_type=jnp.float32),
        "narrow",
        scatter_dimension=0,
        tiled=True,
    )


def normalize(values, gain, shift):
    totals = lax.psum((jnp.sum(values, 1), jnp.sum(values * values, 1)), "narrow")
    row_mean = totals[0] / D
    row_var = totals[1] / D - row_mean * row_mean
    inv_std = lax.rsqrt(row_var + epsilon)
    normed = (values - row_mean[:, None]) * inv_std[:, None]
    return (normed, inv_std, (normed * gain + shift).astype(jnp.bfloat16))


def norm_back(grad, normed, inv_std, gain):
    scaled = grad * gain
    totals = lax.psum((jnp.sum(scaled, 1), jnp.sum(scaled * normed, 1)), "narrow")
    back = inv_std[:, None] * (scaled - totals[0][:, None] / D - normed * (totals[1][:, None] / D))
    return (back, jnp.sum(grad * normed, 0), jnp.sum(grad, 0))


def wide_rows(acts):
    return lax.all_gather(acts, "wide", axis=0, tiled=True)


def narrow_rows(acts):
    return lax.all_gather(acts, "narrow", axis=0, tiled=True)


def wide_sum(partial_rows):
    return lax.psum_scatter(partial_rows, "wide", scatter_dimension=0, tiled=True)


def grad_wide_rows(acts):
    return lax.all_gather(acts, "wide", axis=0, tiled=True)


def grad_narrow_rows(acts):
    return lax.all_gather(acts, "narrow", axis=0, tiled=True)


def grad_wide_sum(partial_rows):
    return lax.psum_scatter(partial_rows, "wide", scatter_dimension=0, tiled=True)


def outer_sum(left, right):
    return lax.dot_general(
        left, right, (((0,), (0,)), ((), ())), preferred_element_type=jnp.float32
    )


def times_trans(left, weight):
    return lax.dot_general(
        left, weight, (((1,), (1,)), ((), ())), preferred_element_type=jnp.float32
    )


def attend(queries, keys_all, values_all, scale):
    scores = (
        jnp.einsum("nqhd,nkhd->nhqk", queries, keys_all, preferred_element_type=jnp.float32) * scale
    )
    top_score = jnp.max(scores, -1, keepdims=True)
    expo = jnp.exp(scores - top_score)
    total = jnp.sum(expo, -1, keepdims=True)
    prob_low = (expo / total).astype(jnp.bfloat16)
    mixed = jnp.einsum("nhqk,nkhd->nqhd", prob_low, values_all, preferred_element_type=jnp.float32)
    return (mixed, top_score + jnp.log(total))


def attend_back(queries, keys_all, values_all, log_total, grad_mixed, scale):
    scores = (
        jnp.einsum("nqhd,nkhd->nhqk", queries, keys_all, preferred_element_type=jnp.float32) * scale
    )
    attn_prob = jnp.exp(scores - log_total)
    grad_values = jnp.einsum(
        "nhqk,nqhd->nkhd",
        attn_prob.astype(jnp.bfloat16),
        grad_mixed,
        preferred_element_type=jnp.float32,
    )
    grad_prob = jnp.einsum(
        "nqhd,nkhd->nhqk", grad_mixed, values_all, preferred_element_type=jnp.float32
    )
    grad_scores = attn_prob * (grad_prob - jnp.sum(grad_prob * attn_prob, -1, keepdims=True))
    grad_scores = grad_scores.astype(jnp.bfloat16)
    grad_queries = (
        jnp.einsum("nhqk,nkhd->nqhd", grad_scores, keys_all, preferred_element_type=jnp.float32)
        * scale
    )
    grad_keys = (
        jnp.einsum("nhqk,nqhd->nkhd", grad_scores, queries, preferred_element_type=jnp.float32)
        * scale
    )
    return (grad_queries, grad_keys, grad_values)


def on_device(
    patches,
    visible,
    w_qkv,
    b_qv,
    w_out,
    b_out,
    w_up,
    b_up,
    w_down,
    b_down,
    gain_one,
    shift_one,
    gain_two,
    shift_two,
    cotangent,
):
    local_images = visible.shape[0]
    narrow_cols = w_qkv.shape[0]
    patch_rows = patches.reshape(local_images, PATCHES, narrow_cols)
    qkv_use, bqv_use, wout_use, wup_use, bup_use, wdown_use = (
        w_qkv,
        b_qv,
        w_out,
        w_up,
        b_up,
        w_down,
    )
    wide_cols = qkv_use.shape[2]
    head_count = wide_cols // HEAD_DIM
    scale = HEAD_DIM ** (-0.5)
    gain_a = gain_one.astype(jnp.float32)
    gain_b = gain_two.astype(jnp.float32)
    w_qkv_flat = qkv_use.reshape(narrow_cols, 3 * wide_cols)
    vis_rows = (
        jnp.take_along_axis(patch_rows, visible[:, :, None], axis=1)
        .reshape(-1, narrow_cols)
        .astype(jnp.float32)
    )
    normed_one, inv_one, hidden_one = normalize(vis_rows, gain_a, shift_one.astype(jnp.float32))
    hidden_one_all = wide_rows(hidden_one)
    bias_row = jnp.concatenate(
        [
            bqv_use[0].astype(jnp.float32),
            jnp.zeros((wide_cols,), jnp.float32),
            bqv_use[1].astype(jnp.float32),
        ]
    )
    triple = (narrow_product(hidden_one_all, w_qkv_flat) + bias_row).astype(jnp.bfloat16)
    image_count = triple.shape[0] // VISIBLE
    split = triple.reshape(image_count, VISIBLE, 3, head_count, HEAD_DIM)
    queries = split[:, :, 0]
    keys_all = split[:, :, 1]
    values_all = split[:, :, 2]
    mixed, log_total = attend(queries, keys_all, values_all, scale)
    mixed = mixed.reshape(-1, wide_cols).astype(jnp.bfloat16)
    mixed_all = narrow_rows(mixed)
    middle = vis_rows + (
        wide_sum(jnp.dot(mixed_all, wout_use, preferred_element_type=jnp.float32))
        + b_out.astype(jnp.float32)
    )
    normed_two, inv_two, hidden_two = normalize(middle, gain_b, shift_two.astype(jnp.float32))
    hidden_two_all = wide_rows(hidden_two)
    inner = narrow_product(hidden_two_all, wup_use) + bup_use.astype(jnp.float32)
    gelu_exact = partial(jax.nn.gelu, approximate=False)
    active = gelu_exact(inner).astype(jnp.bfloat16)
    active_all = narrow_rows(active)
    result = middle + (wide_sum(times_trans(active_all, wdown_use)) + b_down.astype(jnp.float32))
    block_output = result.astype(jnp.bfloat16).reshape(1, -1)
    cot_rows = cotangent.reshape(-1, narrow_cols)
    grad_out = cot_rows.astype(jnp.float32)
    grad_down_all = grad_wide_rows(cot_rows)
    gw_down = outer_sum(grad_down_all, active_all)
    gb_down = jnp.sum(grad_down_all, 0, dtype=jnp.float32)
    grad_active = narrow_product(grad_down_all, wdown_use)
    gelu_pull = jax.vjp(gelu_exact, inner)[1]
    grad_inner = gelu_pull(grad_active)[0].astype(jnp.bfloat16)
    grad_inner_all = grad_narrow_rows(grad_inner)
    gw_up = outer_sum(hidden_two_all, grad_inner_all)
    gb_up = jnp.sum(grad_inner_all, 0, dtype=jnp.float32)
    grad_hidden_two = grad_wide_sum(times_trans(grad_inner_all, wup_use))
    back_two, gg_two, gs_two = norm_back(grad_hidden_two, normed_two, inv_two, gain_b)
    grad_middle = grad_out + back_two
    grad_branch_all = grad_wide_rows(grad_middle.astype(jnp.bfloat16))
    gw_out = outer_sum(mixed_all, grad_branch_all)
    gb_out = jnp.sum(grad_branch_all, 0, dtype=jnp.float32)
    grad_mixed = narrow_product(grad_branch_all, wout_use.T).astype(jnp.bfloat16)
    grad_mixed = grad_mixed.reshape(image_count, VISIBLE, head_count, HEAD_DIM)
    grad_queries, grad_keys, grad_values = attend_back(
        queries, keys_all, values_all, log_total, grad_mixed, scale
    )
    grad_triple = (
        jnp.stack([grad_queries, grad_keys, grad_values], 2)
        .reshape(-1, 3 * wide_cols)
        .astype(jnp.bfloat16)
    )
    grad_triple_all = grad_narrow_rows(grad_triple)
    gw_qkv = outer_sum(hidden_one_all, grad_triple_all).reshape(narrow_cols, 3, wide_cols)
    bias_sums = jnp.sum(grad_triple_all, 0, dtype=jnp.float32).reshape(3, wide_cols)
    gb_qv = jnp.stack([bias_sums[0], bias_sums[2]])
    grad_hidden_one = grad_wide_sum(times_trans(grad_triple_all, w_qkv_flat))
    back_one, gg_one, gs_one = norm_back(grad_hidden_one, normed_one, inv_one, gain_a)
    grad_rows = grad_middle + back_one
    image_index = jnp.arange(local_images)[:, None]
    grad_patches = (
        jnp.zeros((local_images, PATCHES, narrow_cols), jnp.float32)
        .at[image_index, visible]
        .set(grad_rows.reshape(local_images, VISIBLE, narrow_cols))
    )
    grad_patches = grad_patches.reshape(1, -1)
    summed = lax.psum((gw_qkv, gb_qv, gw_out, gb_out, gw_up, gb_up, gw_down, gb_down), "dp")
    vectors = lax.psum((gg_one, gs_one, gg_two, gs_two), ("dp", "wide"))
    return (
        block_output,
        grad_patches,
        summed[0],
        summed[1],
        summed[2],
        summed[3],
        summed[4],
        summed[5],
        summed[6],
        summed[7],
        vectors[0],
        vectors[1],
        vectors[2],
        vectors[3],
    )


def solution(mesh):
    in_specs = (
        P("narrow", ("dp", "wide")),
        P(("dp", "wide"), None),
        P("narrow", None, "wide"),
        P(None, "wide"),
        P("wide", "narrow"),
        P("narrow"),
        P("narrow", "wide"),
        P("wide"),
        P("narrow", "wide"),
        P("narrow"),
        P("narrow"),
        P("narrow"),
        P("narrow"),
        P("narrow"),
        P("narrow", ("dp", "wide")),
    )
    out_specs = (
        P("narrow", ("dp", "wide")),
        P("narrow", ("dp", "wide")),
        P("narrow", None, "wide"),
        P(None, "wide"),
        P("wide", "narrow"),
        P("narrow"),
        P("narrow", "wide"),
        P("wide"),
        P("narrow", "wide"),
        P("narrow"),
        P("narrow"),
        P("narrow"),
        P("narrow"),
        P("narrow"),
    )
    return jax.shard_map(
        on_device, mesh=mesh, in_specs=in_specs, out_specs=out_specs, check_vma=False
    )
```

profile of v0, /device:TPU:0, one launch (start us, length us, event | category | flops | bytes accessed | tf_op | source)
XLA Modules:
  0.0 2732.8 jit_solution(15280021996956817729)
XLA Ops:
  10.3 103.4 %reduce.4 = bf16[2408448]{0:T(1024)(128)(2,1)} reduce(bf16[1,2408448]{1,0:T(2,128)(2,1)} %param.15, bf16[]{:T(256)} %constant.125), dimensions={0}, to_apply=%param.15.reduce_sub_computation | reduce | bytes 9633794 | tf_op args[0]
  126.9 22.3 gather_fusion
  163.7 91.1 %all-gather.11.cloned.1.call-done = bf16[6272,384]{1,0:T(8,128)(2,1)} async-done(((bf16[1568,384]{1,0:T(8,128)(2,1)}), bf16[6272,384]{1,0:T(8,128)(2,1)}) %all-gather.11.cloned.1.call-update) | async-done | bytes 4816912 | tf_op jit(solution)/shard_map/all_gather | solution.py:40
  265.5 179.2 %reduce-scatter.25.cloned.1.call-done = f32[3136,576]{1,0:T(8,128)} async-done(((f32[6272,576]{1,0:T(8,128)}), f32[3136,576]{1,0:T(8,128)}) %reduce-scatter.25.cloned.1.call-update) | async-done | bytes 7225360
  459.3 29.2 %reshape.125 = bf16[64,49,3,3,64]{1,0,4,3,2:T(8,128)(2,1)} reshape(bf16[3136,576]{0,1:T(8,128)(2,1)} %add_convert_fusion.1) | data formatting | bytes 7225344 | tf_op jit(solution)/shard_map/reshape | solution.py:164
  530.0 14.5 reshape.152
  544.6 37.3 %all-gather.23.cloned.1.call-done = bf16[2,3136,192]{1,2,0:T(8,128)(2,1)} async-done(((bf16[1,3136,192]{1,2,0:T(8,128)(2,1)}), bf16[2,3136,192]{1,2,0:T(8,128)(2,1)}) %all-gather.23.cloned.1.call-update) | async-done | bytes 2408464 | tf_op jit(solution)/shard_map/all_gather | solution.py:44
  599.8 26.0 reduce.5
  627.4 136.9 %reduce-scatter.13.cloned.1.call-done = f32[1568,384]{1,0:T(8,128)} async-done(((f32[6272,384]{1,0:T(8,128)}), f32[1568,384]{1,0:T(8,128)}) %reduce-scatter.13.cloned.1.call-update) | async-done | bytes 2408464 | tf_op jit(solution)/shard_map/reduce_scatter | solution.py:48
  779.7 77.9 %all-gather.17.cloned.1.call-done = bf16[6272,384]{1,0:T(8,128)(2,1)} async-done(((bf16[1568,384]{1,0:T(8,128)(2,1)}), bf16[6272,384]{1,0:T(8,128)(2,1)}) %all-gather.17.cloned.1.call-update) | async-done | bytes 4816912 | tf_op jit(solution)/shard_map/all_gather | solution.py:52
  869.2 79.9 %all-gather.13.cloned.1.call-done = bf16[6272,384]{1,0:T(8,128)(2,1)} async-done(((bf16[1568,384]{1,0:T(8,128)(2,1)}), bf16[6272,384]{1,0:T(8,128)(2,1)}) %all-gather.13.cloned.1.call-update) | async-done | bytes 4816912 | tf_op jit(solution)/shard_map/all_gather | solution.py:40
  961.3 204.5 %reduce-scatter.19.cloned.1.call-done = f32[3136,768]{1,0:T(8,128)} async-done(((f32[6272,768]{1,0:T(8,128)}), f32[3136,768]{1,0:T(8,128)}) %reduce-scatter.19.cloned.1.call-update) | async-done | bytes 9633808 | tf_op jit(solution)/shard_map/reduce_scatter | solution.py:15
  1165.8 218.2 %reduce-scatter.15.cloned.1.call-done = f32[3136,768]{1,0:T(8,128)} async-done(((f32[6272,768]{1,0:T(8,128)}), f32[3136,768]{1,0:T(8,128)}) %reduce-scatter.15.cloned.1.call-update) | async-done | bytes 9633808 | tf_op jit(solution)/shard_map/reduce_scatter | solution.py:15
  1384.0 25.5 add_convert_fusion
  1420.7 109.2 %all-gather.19.cloned.1.call-done = bf16[6272,768]{1,0:T(8,128)(2,1)} async-done(((bf16[3136,768]{1,0:T(8,128)(2,1)}), bf16[6272,768]{1,0:T(8,128)(2,1)}) %all-gather.19.cloned.1.call-update) | async-done | bytes 9633808 | tf_op jit(solution)/shard_map/all_gather | solution.py:56
  1541.5 110.0 %all-gather.15.cloned.1.call-done = bf16[6272,768]{1,0:T(8,128)(2,1)} async-done(((bf16[3136,768]{1,0:T(8,128)(2,1)}), bf16[6272,768]{1,0:T(8,128)(2,1)}) %all-gather.15.cloned.1.call-update) | async-done | bytes 9633808 | tf_op jit(solution)/shard_map/all_gather | solution.py:44
  1663.1 155.7 %reduce-scatter.21.cloned.1.call-done = f32[1568,384]{1,0:T(8,128)} async-done(((f32[6272,384]{1,0:T(8,128)}), f32[1568,384]{1,0:T(8,128)}) %reduce-scatter.21.cloned.1.call-update) | async-done | bytes 2408464 | tf_op jit(solution)/shard_map/reduce_scatter | solution.py:60
  1829.8 156.6 %reduce-scatter.17.cloned.1.call-done = f32[1568,384]{1,0:T(8,128)} async-done(((f32[6272,384]{1,0:T(8,128)}), f32[1568,384]{1,0:T(8,128)}) %reduce-scatter.17.cloned.1.call-update) | async-done | bytes 2408464 | tf_op jit(solution)/shard_map/reduce_scatter | solution.py:48
  1991.3 92.0 %all-gather.21.cloned.1.call-done = bf16[6272,384]{1,0:T(8,128)(2,1)} async-done(((bf16[1568,384]{1,0:T(8,128)(2,1)}), bf16[6272,384]{1,0:T(8,128)(2,1)}) %all-gather.21.cloned.1.call-update) | async-done | bytes 4816912 | tf_op jit(solution)/shard_map/all_gather | solution.py:52
  2090.6 76.8 %reduce-scatter.27.cloned.1.call-done = f32[3136,192]{1,0:T(8,128)} async-done(((f32[6272,192]{1,0:T(8,128)}), f32[3136,192]{1,0:T(8,128)}) %reduce-scatter.27.cloned.1.call-update) | async-done | bytes 2408464
  2204.5 13.5 copy.73
  2218.0 15.0 reshape.154
  2257.6 68.1 %all-gather.25.cloned.1.call-done = bf16[2,3136,576]{1,2,0:T(8,128)(2,1)} async-done(((bf16[1,3136,576]{1,2,0:T(8,128)(2,1)}), bf16[2,3136,576]{1,2,0:T(8,128)(2,1)}) %all-gather.25.cloned.1.call-update) | async-done | bytes 7225360 | tf_op jit(solution)/shard_map/all_gather | solution.py:56
  2325.7 39.5 %copy.74 = bf16[2,3136,576]{1,0,2:T(2,128)(2,1)} copy(bf16[2,3136,576]{1,2,0:T(8,128)(2,1)} %all-gather.25.cloned.1.call-done) | data formatting | bytes 14450688 | tf_op jit(solution)/shard_map/all_gather | solution.py:56
  2365.3 11.8 reshape.155
  2420.4 11.7 all-reduce.1
  2432.2 29.8 %all-reduce.9.cloned.1.call-done = (f32[384,3,192]{0,2,1:T(8,128)}, f32[192,384]{1,0:T(8,128)}, f32[384,768]{1,0:T(8,128)}, f32[384,768]{0,1:T(8,128)}) async-done(((f32[384,3,192]{0,2,1:T(8,128)}, f32[192,384]{1,0:T(8,128)}, f32[384,768]{1,0:T(8,128)}, f32[384,768]{0,1:T(8,128)}), (f32[384,3,192]{0,2,1:T(8,128)}, f32[192,384]{1,0:T(8,128)}, f32[384,768]{1,0:T(8,128)}, ...) | async-done | bytes 3538960 | tf_op jit(solution)/shard_map/psum | solution.py:224
  2464.6 164.8 %reduce-scatter.23.cloned.1.call-done = f32[1568,384]{1,0:T(8,128)} async-done(((f32[6272,384]{1,0:T(8,128)}), f32[1568,384]{1,0:T(8,128)}) %reduce-scatter.23.cloned.1.call-update) | async-done | bytes 2408464 | tf_op jit(solution)/shard_map/reduce_scatter | solution.py:60
  2640.5 18.2 scatter_custom_fusion
  2658.7 13.1 copy.75
  2671.8 18.9 reshape.130
  2690.7 32.5 %all-reduce = (f32[384]{0:T(512)}, f32[384]{0:T(512)}, f32[384]{0:T(512)}, f32[384]{0:T(512)}) all-reduce(f32[384]{0:T(512)S(1)} %get-tuple-element.72, f32[384]{0:T(512)S(1)} %get-tuple-element.77, f32[384]{0:T(512)S(1)} %get-tuple-element.70, f32[384]{0:T(512)S(1)} %get-tuple-element.76), channel_id=1, replica_groups=mesh['dp'=4,'wide'=4,'narrow'=2] {'dp','wide'}, use_global_device_ids=true, to_apply=%region_41.42 | all-reduce | flops 1536 | bytes 12288 | tf_op jit(solution)/shard_map/psum | solution.py:225
  (216 shorter events, 334.5 us)
Async XLA Ops:
  7.2 941.9 %copy-start = (bf16[384,768]{1,0:T(8,128)(2,1)S(1)}, bf16[384,768]{1,0:T(8,128)(2,1)}, u32[]{:S(2)}) copy-start(bf16[384,768]{1,0:T(8,128)(2,1)} %param.21) | copy-start | bytes 1769476
  7.2 247.6 %all-gather.11.cloned.1.call-start = ((), (), s32[]{:S(2)}) async-start(), calls=%async_computation.8 | async-start | bytes 6021120 | tf_op jit(solution)/shard_map/all_gather | solution.py:40
  9.4 151.3 %copy-start.27 = (f32[384]{0:T(512)}, f32[384]{0:T(512)S(1)}, u32[]{:S(2)}) copy-start(f32[384]{0:T(512)S(1)} %convert_element_type.103) | copy-start | bytes 4612
  10.2 754.0 %copy-start.25 = (pred[1568]{0:T(1024)(128)(4,1)}, pred[1568]{0:T(1024)(128)(4,1)S(1)}, u32[]{:S(2)}) copy-start(pred[1568]{0:T(1024)(128)(4,1)S(1)} %broadcast_in_dim.20) | copy-start | bytes 4708
  149.2 615.0 %copy-start.3 = (bf16[1568,384]{1,0:T(8,128)(2,1)}, bf16[1568,384]{1,0:T(8,128)(2,1)S(1)}, u32[]{:S(2)}) copy-start(bf16[1568,384]{1,0:T(8,128)(2,1)S(1)} %gather_fusion) | copy-start | bytes 3612676
  163.4 281.3 %reduce-scatter.25.cloned.1.call-start = ((), (), s32[]{:S(2)}) async-start(), calls=%async_computation.22 | async-start | bytes 24084480
  264.7 317.2 %all-gather.23.cloned.1.call-start = ((), (), s32[]{:S(2)}) async-start(), calls=%async_computation.20 | async-start | bytes 3686400 | tf_op jit(solution)/shard_map/all_gather | solution.py:44
  544.6 219.6 %reduce-scatter.13.cloned.1.call-start = ((), (), s32[]{:S(2)}) async-start(), calls=%async_computation.9 | async-start | bytes 12042240 | tf_op jit(solution)/shard_map/reduce_scatter | solution.py:48
  599.7 257.9 %all-gather.17.cloned.1.call-start = ((), (), s32[]{:S(2)}) async-start(), calls=%async_computation.14 | async-start | bytes 6021120 | tf_op jit(solution)/shard_map/all_gather | solution.py:52
  627.2 321.9 %all-gather.13.cloned.1.call-start = ((), (), s32[]{:S(2)}) async-start(), calls=%async_computation.10 | async-start | bytes 6021120 | tf_op jit(solution)/shard_map/all_gather | solution.py:40
  627.4 230.2 %copy-start.16 = (bf16[384,768]{1,0:T(8,128)(2,1)S(1)}, bf16[384,768]{1,0:T(8,128)(2,1)}, u32[]{:S(2)}) copy-start(bf16[384,768]{1,0:T(8,128)(2,1)} %param.23) | copy-start | bytes 1769476
  779.7 386.1 %reduce-scatter.19.cloned.1.call-start = ((), (), s32[]{:S(2)}) async-start(), calls=%async_computation.15 | async-start | bytes 28901376 | tf_op jit(solution)/shard_map/reduce_scatter | solution.py:15
  869.1 514.9 %reduce-scatter.15.cloned.1.call-start = ((), (), s32[]{:S(2)}) async-start(), calls=%async_computation.11 | async-start | bytes 28901376 | tf_op jit(solution)/shard_map/reduce_scatter | solution.py:15
  960.6 569.2 %all-gather.19.cloned.1.call-start = ((), (), s32[]{:S(2)}) async-start(), calls=%async_computation.16 | async-start | bytes 14450688 | tf_op jit(solution)/shard_map/all_gather | solution.py:56
  1409.6 241.9 %all-gather.15.cloned.1.call-start = ((), (), s32[]{:S(2)}) async-start(), calls=%async_computation.12 | async-start | bytes 14450688 | tf_op jit(solution)/shard_map/all_gather | solution.py:44
  1420.7 398.2 %reduce-scatter.21.cloned.1.call-start = ((), (), s32[]{:S(2)}) async-start(), calls=%async_computation.17 | async-start | bytes 12042240 | tf_op jit(solution)/shard_map/reduce_scatter | solution.py:60
  1541.4 445.0 %reduce-scatter.17.cloned.1.call-start = ((), (), s32[]{:S(2)}) async-start(), calls=%async_computation.13 | async-start | bytes 12042240 | tf_op jit(solution)/shard_map/reduce_scatter | solution.py:48
  1662.5 156.4 %copy-start.5 = (f32[1568,384]{1,0:T(8,128)S(1)}, f32[1568,384]{1,0:T(8,128)}, u32[]{:S(2)}) copy-start(f32[1568,384]{1,0:T(8,128)} %get-tuple-element.106) | copy-start | bytes 7225348
  1662.5 420.9 %all-gather.21.cloned.1.call-start = ((), (), s32[]{:S(2)}) async-start(), calls=%async_computation.18 | async-start | bytes 6021120 | tf_op jit(solution)/shard_map/all_gather | solution.py:52
  1991.3 176.1 %reduce-scatter.27.cloned.1.call-start = ((), (), s32[]{:S(2)}) async-start(), calls=%async_computation.23 | async-start | bytes 9633792
  2090.4 235.4 %all-gather.25.cloned.1.call-start = ((), (), s32[]{:S(2)}) async-start(), calls=%async_computation.21 | async-start | bytes 11059200 | tf_op jit(solution)/shard_map/all_gather | solution.py:56
  2233.0 228.9 %all-reduce.9.cloned.1.call-start = ((), (), s32[]{:S(2)}) async-start(), calls=%async_computation.24 | async-start | bytes 7077888 | tf_op jit(solution)/shard_map/psum | solution.py:224
  2386.4 243.0 %reduce-scatter.23.cloned.1.call-start = ((), (), s32[]{:S(2)}) async-start(), calls=%async_computation.19 | async-start | bytes 12042240 | tf_op jit(solution)/shard_map/reduce_scatter | solution.py:60
  2419.3 210.1 %copy-start.4 = (bf16[1568,384]{1,0:T(8,128)(2,1)S(1)}, bf16[1568,384]{1,0:T(8,128)(2,1)}, u32[]{:S(2)}) copy-start(bf16[1568,384]{1,0:T(8,128)(2,1)} %copy-done.3) | copy-start | bytes 3612676
  2419.3 210.1 %copy-start.22 = (f32[1568]{0:T(1024)S(1)}, f32[1568]{0:T(1024)}, u32[]{:S(2)}) copy-start(f32[1568]{0:T(1024)} %copy-done.21) | copy-start | bytes 18820
  2419.3 210.1 %copy-start.24 = (f32[1568]{0:T(1024)S(1)}, f32[1568]{0:T(1024)}, u32[]{:S(2)}) copy-start(f32[1568]{0:T(1024)} %copy-done.23) | copy-start | bytes 18820
  2419.3 210.1 %copy-start.26 = (pred[1568]{0:T(1024)(128)(4,1)S(1)}, pred[1568]{0:T(1024)(128)(4,1)}, u32[]{:S(2)}) copy-start(pred[1568]{0:T(1024)(128)(4,1)} %copy-done.25) | copy-start | bytes 4708
  2419.4 210.1 %copy-start.28 = (f32[384]{0:T(512)S(1)}, f32[384]{0:T(512)}, u32[]{:S(2)}) copy-start(f32[384]{0:T(512)} %copy-done.27) | copy-start | bytes 4612
  2671.8 51.4 %copy-start.15 = (f32[384,3,192]{0,2,1:T(8,128)S(1)}, f32[384,3,192]{0,2,1:T(8,128)}, u32[]{:S(2)}) copy-start(f32[384,3,192]{0,2,1:T(8,128)} %get-tuple-element.127) | copy-start | bytes 2654212
  2671.8 52.3 %copy-start.19 = (f32[192,384]{1,0:T(8,128)S(1)}, f32[192,384]{1,0:T(8,128)}, u32[]{:S(2)}) copy-start(f32[192,384]{1,0:T(8,128)} %get-tuple-element.129) | copy-start | bytes 884740
  2671.8 53.0 %copy-start.14 = (f32[384,768]{1,0:T(8,128)S(1)}, f32[384,768]{1,0:T(8,128)}, u32[]{:S(2)}) copy-start(f32[384,768]{1,0:T(8,128)} %get-tuple-element.131) | copy-start | bytes 3538948
  2671.8 54.0 %copy-start.1 = (bf16[384,768]{1,0:T(8,128)(2,1)S(1)}, bf16[384,768]{1,0:T(8,128)(2,1)}, u32[]{:S(2)}) copy-start(bf16[384,768]{1,0:T(8,128)(2,1)} %param.21) | copy-start | bytes 1769476
  (30 other events, 319.0 us)
Sparse Core Ops, SparseCore 0:
  163.5 91.2 all-gather.10
  264.9 179.8 reduce-scatter.24
  544.7 37.1 all-gather.22
  599.8 164.3 reduce-scatter.12
  765.6 91.9 all-gather.16
  859.6 89.4 all-gather.12
  951.4 214.3 reduce-scatter.18
  1168.1 215.8 reduce-scatter.14
  1409.7 120.1 all-gather.18
  1531.3 120.1 all-gather.14
  1654.4 164.3 reduce-scatter.20
  1821.1 165.2 reduce-scatter.16
  1991.4 91.9 all-gather.20
  2090.5 76.8 reduce-scatter.26
  2233.2 92.5 all-gather.24
  2386.6 75.3 all-reduce.8
  2464.9 164.4 reduce-scatter.22
where the time goes:
time: 2740 us; the launch traced here: 2730 us
  waiting for transfers between devices  1990 us (73%)
  local copies, waits for them, and re-layouts  283 us (10%)
  other arithmetic  233 us (9%)
  matrix products  134 us (5%)
  blocking collectives  78.4 us (3%)
    reduce_scatter x2, waiting for transfers between devices, narrow_product(): lax.psum_scatter(jnp.dot(acts, weight, preferred_element_type=jnp.float32...  423 us
    reduce_scatter x2, waiting for transfers between devices, grad_wide_sum(): lax.psum_scatter(partial_rows, 'wide', scatter_dimension=0, tiled=True)  320 us
    reduce_scatter x2, waiting for transfers between devices, wide_sum(): lax.psum_scatter(partial_rows, 'wide', scatter_dimension=0, tiled=True)  294 us
    unnamed x19, waiting for transfers between devices  256 us
    all_gather x2, waiting for transfers between devices, grad_narrow_rows(): return lax.all_gather(acts, 'narrow', axis=0, tiled=True)  177 us
    all_gather x2, waiting for transfers between devices, wide_rows(): return lax.all_gather(acts, 'wide', axis=0, tiled=True)  171 us
    all_gather x2, waiting for transfers between devices, grad_wide_rows(): return lax.all_gather(acts, 'wide', axis=0, tiled=True)  170 us
    unnamed x10, other arithmetic  148 us
  transfers between devices with their start and end apart: 17, of which 17 were waited for; matrix products, arithmetic and copies ran while one was open for 6% of the time, Pallas kernels for 0%

commit v1 on v0

--- a/solution.py
+++ b/solution.py
@@ -9,6 +9,28 @@
 PATCHES = 196
 VISIBLE = 49
 epsilon = 1e-06
+
+
+def joined_along(tiles, dim):
+    tiles = jnp.moveaxis(tiles, 0, dim)
+    shape = tiles.shape
+    return tiles.reshape(*shape[:dim], shape[dim] * shape[dim + 1], *shape[dim + 2 :])
+
+
+def grow_blocks(value, axis):
+    size = lax.axis_size(axis)
+    blocks = value[None]
+    for level in range(size.bit_length() - 1):
+        bit = 1 << level
+        theirs = lax.ppermute(blocks, axis, [(i, i ^ bit) for i in range(size)])
+        both = jnp.stack([blocks, theirs])
+        upper = lax.axis_index(axis) >> level & 1
+        blocks = jnp.where(upper == 0, both, both[::-1]).reshape(-1, *value.shape)
+    return blocks
+
+
+def gather_by_bits(value, axis, dim):
+    return joined_along(grow_blocks(value, axis), dim)
 
 
 def narrow_product(acts, weight):
@@ -41,7 +63,7 @@
 
 
 def narrow_rows(acts):
-    return lax.all_gather(acts, "narrow", axis=0, tiled=True)
+    return gather_by_bits(acts, "narrow", 0)
 
 
 def wide_sum(partial_rows):

time: 2740 us -> 2620 us (0.956)
  waiting for transfers between devices: 1990 us -> 1830 us
  other arithmetic: 233 us -> 266 us
    all_gather x2 -> x0, waiting for transfers between devices: 147 us -> none  [narrow_rows(): return lax.all_gather(acts, 'narrow', axis=0, tiled=True)]
    reduce_scatter x2, waiting for transfers between devices: 320 us -> 180 us  [grad_wide_sum(): lax.psum_scatter(partial_rows, 'wide', scatter_dimension=0, tiled=True)]
    ppermute x0 -> x2, waiting for transfers between devices: none -> 119 us  [grow_blocks(): theirs = lax.ppermute(blocks, axis, [(i, i ^ bit) for i in range(size)])]
    unnamed x105 -> x103, local copies, waits for them, and re-layouts: 97.1 us -> 78 us
    unnamed x19 -> x17, waiting for transfers between devices: 256 us -> 256 us
  transfers between devices with their start and end apart: 17 -> 17, of which waited for: 17 -> 17; matrix products, arithmetic and copies ran while one was open for 6% -> 7% of each run, Pallas kernels for 0% -> 0%
where the time goes in v1:
time: 2620 us; the launch traced here: 2600 us
  waiting for transfers between devices  1830 us (70%)
  local copies, waits for them, and re-layouts  279 us (11%)
  other arithmetic  266 us (10%)
  matrix products  134 us (5%)
  blocking collectives  78 us (3%)
    reduce_scatter x2, waiting for transfers between devices, narrow_product(): lax.psum_scatter(jnp.dot(acts, weight, preferred_element_type=jnp.float32...  423 us
    reduce_scatter x2, waiting for transfers between devices, wide_sum(): lax.psum_scatter(partial_rows, 'wide', scatter_dimension=0, tiled=True)  294 us
    unnamed x17, waiting for transfers between devices  256 us
    all_gather x2, waiting for transfers between devices, grad_narrow_rows(): return lax.all_gather(acts, 'narrow', axis=0, tiled=True)  188 us
    reduce_scatter x2, waiting for transfers between devices, grad_wide_sum(): lax.psum_scatter(partial_rows, 'wide', scatter_dimension=0, tiled=True)  180 us
    all_gather x2, waiting for transfers between devices, wide_rows(): return lax.all_gather(acts, 'wide', axis=0, tiled=True)  171 us
    all_gather x2, waiting for transfers between devices, grad_wide_rows(): return lax.all_gather(acts, 'wide', axis=0, tiled=True)  170 us
    unnamed x10, other arithmetic  148 us
  transfers between devices with their start and end apart: 17, of which 17 were waited for; matrix products, arithmetic and copies ran while one was open for 7% of the time, Pallas kernels for 0%

profile of v1, /device:TPU:0, one launch (start us, length us, event | category | flops | bytes accessed | tf_op | source)
XLA Modules:
  0.0 2604.3 jit_solution(17130178608924197324)
XLA Ops:
  10.3 103.4 %reduce.4 = bf16[2408448]{0:T(1024)(128)(2,1)} reduce(bf16[1,2408448]{1,0:T(2,128)(2,1)} %param.15, bf16[]{:T(256)} %constant.132), dimensions={0}, to_apply=%param.15.reduce_sub_computation | reduce | bytes 9633794 | tf_op args[0]
  126.9 22.3 gather_fusion
  163.6 91.2 %all-gather.8.cloned.1.call-done = bf16[6272,384]{1,0:T(8,128)(2,1)} async-done(((bf16[1568,384]{1,0:T(8,128)(2,1)}), bf16[6272,384]{1,0:T(8,128)(2,1)}) %all-gather.8.cloned.1.call-update) | async-done | bytes 4816912 | tf_op jit(solution)/shard_map/all_gather | solution.py:62
  265.4 179.2 %reduce-scatter.25.cloned.1.call-done = f32[3136,576]{1,0:T(8,128)} async-done(((f32[6272,576]{1,0:T(8,128)}), f32[3136,576]{1,0:T(8,128)}) %reduce-scatter.25.cloned.1.call-update) | async-done | bytes 7225360
  459.2 29.2 %reshape.146 = bf16[64,49,3,3,64]{1,0,4,3,2:T(8,128)(2,1)} reshape(bf16[3136,576]{0,1:T(8,128)(2,1)} %add_convert_fusion.1) | data formatting | bytes 7225344 | tf_op jit(solution)/shard_map/reshape | solution.py:186
  541.8 23.6 collective-permute-done
  583.5 26.2 %reduce.5 = bf16[602112]{0:T(1024)(128)(2,1)S(1)} reduce(bf16[1,602112]{1,0:T(2,128)(2,1)} %param.29, bf16[]{:T(256)} %constant.132), dimensions={0}, to_apply=%param.29.reduce_sub_computation | reduce | bytes 2408450 | tf_op args[14]
  611.3 136.7 %reduce-scatter.13.cloned.1.call-done = f32[1568,384]{1,0:T(8,128)} async-done(((f32[6272,384]{1,0:T(8,128)}), f32[1568,384]{1,0:T(8,128)}) %reduce-scatter.13.cloned.1.call-update) | async-done | bytes 2408464 | tf_op jit(solution)/shard_map/reduce_scatter | solution.py:70
  763.2 78.2 %all-gather.12.cloned.1.call-done = bf16[6272,384]{1,0:T(8,128)(2,1)} async-done(((bf16[1568,384]{1,0:T(8,128)(2,1)}), bf16[6272,384]{1,0:T(8,128)(2,1)}) %all-gather.12.cloned.1.call-update) | async-done | bytes 4816912 | tf_op jit(solution)/shard_map/all_gather | solution.py:74
  853.0 79.8 %all-gather.10.cloned.1.call-done = bf16[6272,384]{1,0:T(8,128)(2,1)} async-done(((bf16[1568,384]{1,0:T(8,128)(2,1)}), bf16[6272,384]{1,0:T(8,128)(2,1)}) %all-gather.10.cloned.1.call-update) | async-done | bytes 4816912 | tf_op jit(solution)/shard_map/all_gather | solution.py:62
  945.1 204.3 %reduce-scatter.19.cloned.1.call-done = f32[3136,768]{1,0:T(8,128)} async-done(((f32[6272,768]{1,0:T(8,128)}), f32[3136,768]{1,0:T(8,128)}) %reduce-scatter.19.cloned.1.call-update) | async-done | bytes 9633808 | tf_op jit(solution)/shard_map/reduce_scatter | solution.py:37
  1149.4 218.2 %reduce-scatter.15.cloned.1.call-done = f32[3136,768]{1,0:T(8,128)} async-done(((f32[6272,768]{1,0:T(8,128)}), f32[3136,768]{1,0:T(8,128)}) %reduce-scatter.15.cloned.1.call-update) | async-done | bytes 9633808 | tf_op jit(solution)/shard_map/reduce_scatter | solution.py:37
  1367.6 25.8 add_convert_fusion
  1393.5 120.3 %all-gather.14.cloned.1.call-done = bf16[6272,768]{1,0:T(8,128)(2,1)} async-done(((bf16[3136,768]{1,0:T(8,128)(2,1)}), bf16[6272,768]{1,0:T(8,128)(2,1)}) %all-gather.14.cloned.1.call-update) | async-done | bytes 9633808 | tf_op jit(solution)/shard_map/all_gather | solution.py:78
  1545.6 95.5 %collective-permute-done.1 = bf16[1,3136,768]{2,1,0:T(8,128)(2,1)} collective-permute-done((bf16[1,3136,768]{2,1,0:T(8,128)(2,1)}, bf16[1,3136,768]{2,1,0:T(8,128)(2,1)}, u32[]{:S(2)}, u32[]{:S(2)}) %collective-permute-start.1) | collective-permute-done | bytes 4816928 | tf_op jit(solution)/shard_map/ppermute | solution.py:25
  1649.7 12.4 reverse_select_fusion
  1674.1 15.4 reduce-scatter.21.cloned.1.call-done
  1700.4 157.2 %reduce-scatter.17.cloned.1.call-done = f32[1568,384]{1,0:T(8,128)} async-done(((f32[6272,384]{1,0:T(8,128)}), f32[1568,384]{1,0:T(8,128)}) %reduce-scatter.17.cloned.1.call-update) | async-done | bytes 2408464 | tf_op jit(solution)/shard_map/reduce_scatter | solution.py:70
  1862.5 92.0 %all-gather.16.cloned.1.call-done = bf16[6272,384]{1,0:T(8,128)(2,1)} async-done(((bf16[1568,384]{1,0:T(8,128)(2,1)}), bf16[6272,384]{1,0:T(8,128)(2,1)}) %all-gather.16.cloned.1.call-update) | async-done | bytes 4816912 | tf_op jit(solution)/shard_map/all_gather | solution.py:74
  1961.7 77.0 %reduce-scatter.27.cloned.1.call-done = f32[3136,192]{1,0:T(8,128)} async-done(((f32[6272,192]{1,0:T(8,128)}), f32[3136,192]{1,0:T(8,128)}) %reduce-scatter.27.cloned.1.call-update) | async-done | bytes 2408464
  2075.9 13.5 copy.76
  2089.4 15.0 reshape.173
  2129.0 68.2 %all-gather.18.cloned.1.call-done = bf16[2,3136,576]{1,2,0:T(8,128)(2,1)} async-done(((bf16[1,3136,576]{1,2,0:T(8,128)(2,1)}), bf16[2,3136,576]{1,2,0:T(8,128)(2,1)}) %all-gather.18.cloned.1.call-update) | async-done | bytes 7225360 | tf_op jit(solution)/shard_map/all_gather | solution.py:78
  2197.2 39.5 %copy.77 = bf16[2,3136,576]{1,0,2:T(2,128)(2,1)} copy(bf16[2,3136,576]{1,2,0:T(8,128)(2,1)} %all-gather.18.cloned.1.call-done) | data formatting | bytes 14450688 | tf_op jit(solution)/shard_map/all_gather | solution.py:78
  2236.7 11.8 reshape.174
  2291.9 11.7 all-reduce.1
  2303.6 29.8 %all-reduce.9.cloned.1.call-done = (f32[384,3,192]{0,2,1:T(8,128)}, f32[192,384]{1,0:T(8,128)}, f32[384,768]{1,0:T(8,128)}, f32[384,768]{0,1:T(8,128)}) async-done(((f32[384,3,192]{0,2,1:T(8,128)}, f32[192,384]{1,0:T(8,128)}, f32[384,768]{1,0:T(8,128)}, f32[384,768]{0,1:T(8,128)}), (f32[384,3,192]{0,2,1:T(8,128)}, f32[192,384]{1,0:T(8,128)}, f32[384,768]{1,0:T(8,128)}, ...) | async-done | bytes 3538960 | tf_op jit(solution)/shard_map/psum | solution.py:246
  2336.1 164.8 %reduce-scatter.23.cloned.1.call-done = f32[1568,384]{1,0:T(8,128)} async-done(((f32[6272,384]{1,0:T(8,128)}), f32[1568,384]{1,0:T(8,128)}) %reduce-scatter.23.cloned.1.call-update) | async-done | bytes 2408464 | tf_op jit(solution)/shard_map/reduce_scatter | solution.py:82
  2512.0 18.2 scatter_custom_fusion
  2530.2 13.1 copy.78
  2543.3 18.9 reshape.151
  2562.1 32.5 %all-reduce = (f32[384]{0:T(512)}, f32[384]{0:T(512)}, f32[384]{0:T(512)}, f32[384]{0:T(512)}) all-reduce(f32[384]{0:T(512)S(1)} %get-tuple-element.72, f32[384]{0:T(512)S(1)} %get-tuple-element.77, f32[384]{0:T(512)S(1)} %get-tuple-element.70, f32[384]{0:T(512)S(1)} %get-tuple-element.76), channel_id=1, replica_groups=mesh['dp'=4,'wide'=4,'narrow'=2] {'dp','wide'}, use_global_device_ids=true, to_apply=%region_41.42 | all-reduce | flops 1536 | bytes 12288 | tf_op jit(solution)/shard_map/psum | solution.py:247
  (220 shorter events, 364.3 us)
Async XLA Ops:
  7.2 925.7 %copy-start = (bf16[384,768]{1,0:T(8,128)(2,1)S(1)}, bf16[384,768]{1,0:T(8,128)(2,1)}, u32[]{:S(2)}) copy-start(bf16[384,768]{1,0:T(8,128)(2,1)} %param.21) | copy-start | bytes 1769476
  7.2 247.6 %all-gather.8.cloned.1.call-start = ((), (), s32[]{:S(2)}) async-start(), calls=%async_computation.8 | async-start | bytes 6021120 | tf_op jit(solution)/shard_map/all_gather | solution.py:62
  9.4 151.2 %copy-start.27 = (f32[384]{0:T(512)}, f32[384]{0:T(512)S(1)}, u32[]{:S(2)}) copy-start(f32[384]{0:T(512)S(1)} %convert_element_type.121) | copy-start | bytes 4612
  10.2 737.8 %copy-start.25 = (pred[1568]{0:T(1024)(128)(4,1)}, pred[1568]{0:T(1024)(128)(4,1)S(1)}, u32[]{:S(2)}) copy-start(pred[1568]{0:T(1024)(128)(4,1)S(1)} %broadcast_in_dim.22) | copy-start | bytes 4708
  149.1 598.8 %copy-start.3 = (bf16[1568,384]{1,0:T(8,128)(2,1)}, bf16[1568,384]{1,0:T(8,128)(2,1)S(1)}, u32[]{:S(2)}) copy-start(bf16[1568,384]{1,0:T(8,128)(2,1)S(1)} %gather_fusion) | copy-start | bytes 3612676
  163.3 281.4 %reduce-scatter.25.cloned.1.call-start = ((), (), s32[]{:S(2)}) async-start(), calls=%async_computation.20 | async-start | bytes 24084480
  264.7 483.3 %reduce-scatter.13.cloned.1.call-start = ((), (), s32[]{:S(2)}) async-start(), calls=%async_computation.9 | async-start | bytes 12042240 | tf_op jit(solution)/shard_map/reduce_scatter | solution.py:70
  536.3 29.1 %collective-permute-start = (bf16[1,3136,192]{1,2,0:T(8,128)(2,1)}, bf16[1,3136,192]{1,2,0:T(8,128)(2,1)}, u32[]{:S(2)}, u32[]{:S(2)}) collective-permute-start(bf16[1,3136,192]{1,2,0:T(8,128)(2,1)} %convert_element_type.133), channel_id=1, source_target_pairs={{0,1},{1,0},{2,3},{3,2},{4,5},{5,4},{6,7},{7,6},{8,9},{9,8},{10,11... | collective-permute-start | bytes 3612680 | tf_op jit(solution)/shard_map/ppermute | solution.py:25
  583.4 27.8 %copy-start.33 = (bf16[384]{0:T(512)(128)(2,1)S(1)}, bf16[384]{0:T(512)(128)(2,1)}, u32[]{:S(2)}) copy-start(bf16[384]{0:T(512)(128)(2,1)} %param.28) | copy-start | bytes 2308
  583.5 257.9 %all-gather.12.cloned.1.call-start = ((), (), s32[]{:S(2)}) async-start(), calls=%async_computation.13 | async-start | bytes 6021120 | tf_op jit(solution)/shard_map/all_gather | solution.py:74
  611.1 321.7 %all-gather.10.cloned.1.call-start = ((), (), s32[]{:S(2)}) async-start(), calls=%async_computation.10 | async-start | bytes 6021120 | tf_op jit(solution)/shard_map/all_gather | solution.py:62
  611.3 230.1 %copy-start.16 = (bf16[384,768]{1,0:T(8,128)(2,1)S(1)}, bf16[384,768]{1,0:T(8,128)(2,1)}, u32[]{:S(2)}) copy-start(bf16[384,768]{1,0:T(8,128)(2,1)} %param.23) | copy-start | bytes 1769476
  763.1 386.3 %reduce-scatter.19.cloned.1.call-start = ((), (), s32[]{:S(2)}) async-start(), calls=%async_computation.14 | async-start | bytes 28901376 | tf_op jit(solution)/shard_map/reduce_scatter | solution.py:37
  853.0 514.7 %reduce-scatter.15.cloned.1.call-start = ((), (), s32[]{:S(2)}) async-start(), calls=%async_computation.11 | async-start | bytes 28901376 | tf_op jit(solution)/shard_map/reduce_scatter | solution.py:37
  944.4 569.3 %all-gather.14.cloned.1.call-start = ((), (), s32[]{:S(2)}) async-start(), calls=%async_computation.15 | async-start | bytes 14450688 | tf_op jit(solution)/shard_map/all_gather | solution.py:78
  1393.5 296.1 %reduce-scatter.21.cloned.1.call-start = ((), (), s32[]{:S(2)}) async-start(), calls=%async_computation.16 | async-start | bytes 12042240 | tf_op jit(solution)/shard_map/reduce_scatter | solution.py:82
  1525.0 332.7 %reduce-scatter.17.cloned.1.call-start = ((), (), s32[]{:S(2)}) async-start(), calls=%async_computation.12 | async-start | bytes 12042240 | tf_op jit(solution)/shard_map/reduce_scatter | solution.py:70
  1535.5 105.6 %collective-permute-start.1 = (bf16[1,3136,768]{2,1,0:T(8,128)(2,1)}, bf16[1,3136,768]{2,1,0:T(8,128)(2,1)}, u32[]{:S(2)}, u32[]{:S(2)}) collective-permute-start(bf16[1,3136,768]{2,1,0:T(8,128)(2,1)} %fusion.107), channel_id=1, source_target_pairs={{0,1},{1,0},{2,3},{3,2},{4,5},{5,4},{6,7},{7,6},{8,9},{9,8},{10,11... | collective-permute-start | bytes 14450696 | tf_op jit(solution)/shard_map/ppermute | solution.py:25
  1673.4 281.1 %all-gather.16.cloned.1.call-start = ((), (), s32[]{:S(2)}) async-start(), calls=%async_computation.17 | async-start | bytes 6021120 | tf_op jit(solution)/shard_map/all_gather | solution.py:74
  1862.5 176.1 %reduce-scatter.27.cloned.1.call-start = ((), (), s32[]{:S(2)}) async-start(), calls=%async_computation.21 | async-start | bytes 9633792
  1961.6 235.6 %all-gather.18.cloned.1.call-start = ((), (), s32[]{:S(2)}) async-start(), calls=%async_computation.19 | async-start | bytes 11059200 | tf_op jit(solution)/shard_map/all_gather | solution.py:78
  2104.5 229.0 %all-reduce.9.cloned.1.call-start = ((), (), s32[]{:S(2)}) async-start(), calls=%async_computation.22 | async-start | bytes 7077888 | tf_op jit(solution)/shard_map/psum | solution.py:246
  2257.9 243.0 %reduce-scatter.23.cloned.1.call-start = ((), (), s32[]{:S(2)}) async-start(), calls=%async_computation.18 | async-start | bytes 12042240 | tf_op jit(solution)/shard_map/reduce_scatter | solution.py:82
  2290.7 210.1 %copy-start.4 = (bf16[1568,384]{1,0:T(8,128)(2,1)S(1)}, bf16[1568,384]{1,0:T(8,128)(2,1)}, u32[]{:S(2)}) copy-start(bf16[1568,384]{1,0:T(8,128)(2,1)} %copy-done.3) | copy-start | bytes 3612676
  2290.7 210.1 %copy-start.22 = (f32[1568]{0:T(1024)S(1)}, f32[1568]{0:T(1024)}, u32[]{:S(2)}) copy-start(f32[1568]{0:T(1024)} %copy-done.21) | copy-start | bytes 18820
  2290.8 210.1 %copy-start.24 = (f32[1568]{0:T(1024)S(1)}, f32[1568]{0:T(1024)}, u32[]{:S(2)}) copy-start(f32[1568]{0:T(1024)} %copy-done.23) | copy-start | bytes 18820
  2290.8 210.1 %copy-start.26 = (pred[1568]{0:T(1024)(128)(4,1)S(1)}, pred[1568]{0:T(1024)(128)(4,1)}, u32[]{:S(2)}) copy-start(pred[1568]{0:T(1024)(128)(4,1)} %copy-done.25) | copy-start | bytes 4708
  2290.8 210.1 %copy-start.28 = (f32[384]{0:T(512)S(1)}, f32[384]{0:T(512)}, u32[]{:S(2)}) copy-start(f32[384]{0:T(512)} %copy-done.27) | copy-start | bytes 4612
  2543.3 51.4 %copy-start.15 = (f32[384,3,192]{0,2,1:T(8,128)S(1)}, f32[384,3,192]{0,2,1:T(8,128)}, u32[]{:S(2)}) copy-start(f32[384,3,192]{0,2,1:T(8,128)} %get-tuple-element.127) | copy-start | bytes 2654212
  2543.3 52.3 %copy-start.19 = (f32[192,384]{1,0:T(8,128)S(1)}, f32[192,384]{1,0:T(8,128)}, u32[]{:S(2)}) copy-start(f32[192,384]{1,0:T(8,128)} %get-tuple-element.129) | copy-start | bytes 884740
  2543.3 53.0 %copy-start.14 = (f32[384,768]{1,0:T(8,128)S(1)}, f32[384,768]{1,0:T(8,128)}, u32[]{:S(2)}) copy-start(f32[384,768]{1,0:T(8,128)} %get-tuple-element.131) | copy-start | bytes 3538948
  2543.3 54.0 %copy-start.1 = (bf16[384,768]{1,0:T(8,128)(2,1)S(1)}, bf16[384,768]{1,0:T(8,128)(2,1)}, u32[]{:S(2)}) copy-start(bf16[384,768]{1,0:T(8,128)(2,1)} %param.21) | copy-start | bytes 1769476
  (30 other events, 268.8 us)
Sparse Core Ops, SparseCore 0:
  163.4 91.3 all-gather.7
  264.8 179.8 reduce-scatter.24
  583.5 164.3 reduce-scatter.12
  749.4 91.9 all-gather.11
  843.4 89.4 all-gather.9
  935.0 214.3 reduce-scatter.18
  1151.7 215.8 reduce-scatter.14
  1393.6 120.1 all-gather.13
  1525.1 164.3 reduce-scatter.20
  1692.3 165.2 reduce-scatter.16
  1862.6 91.9 all-gather.15
  1961.7 76.8 reduce-scatter.26
  2104.6 92.5 all-gather.17
  2258.0 75.3 all-reduce.8
  2336.3 164.4 reduce-scatter.22
